TPU v7x, 256 devices: a whole 4x4x8 slice. The times are simulated.
256 devices in a mesh: gx: 32 (over z, x_hi, core), gy: 8 (over y, x_lo).
Axes of the slice: x: 4 (x_hi: 2, x_lo: 2; x = x_hi * 2 + x_lo), y: 4, z: 8, core: 2. Of those that a mesh axis runs over, the one named last changes fastest.
Arguments:
- features: bfloat16 [32, 8, 3, 64, 256], P('gx', 'gy'), may hold values from -6 to 6
- block_coords: int32 [32, 8, 3], P('gx', 'gy'), may hold values from 0 to 31, as said below
- block_counts: int32 [32, 8], P('gx', 'gy'), may hold values from 2 to 3, as said below
- first_weight: bfloat16 [6912, 256], replicated, may hold values from -0.078125 to 0.078125
- second_weight: bfloat16 [6912, 256], replicated, may hold values from -0.078125 to 0.078125
- cotangent: bfloat16 [32, 8, 3, 64, 256], P('gx', 'gy'), may hold values from -6 to 6
Outputs:
- output_features: float32 [32, 8, 3, 64, 256], P('gx', 'gy')
- input_grad: float32 [32, 8, 3, 64, 256], P('gx', 'gy')
- first_weight_grad: float32 [6912, 256], P('gx', 'gy')
- second_weight_grad: float32 [6912, 256], P('gx', 'gy')
Inputs may be any that keep to these rules, and one draw needn't show every extreme that they name: `block_coords`: within a tile all 3 entries are distinct block positions, so slots at or past the tile's count name blocks that are not active. Slots 0 and 1 are always live and hold blocks of the lowest block layer in opposite corners of the tile's 2 x 2 block columns. `block_counts`: at least one tile holds 3 live slots in every draw.
All inputs are finite; a program needn't handle non-finite values.
Results may differ from a plain program's by a relative error of at most 0.0029.
Values may be sent and summed in bfloat16 or wider, within the bound.
A program may use at most 128 MiB of HBM per device.

v0:
```python
import functools
import math

import jax
import jax.numpy as jnp
import numpy as np
from jax import lax
from jax.experimental import pallas as pl
from jax.experimental.pallas import tpu as pltpu
from jax.sharding import PartitionSpec as P

C = 256
SLOTS = 3
ROWS = 192
FACE = 256
DATA = FACE + ROWS
DEAD = -(1 << 24)
LIMIT = 56 << 20
MESH = pl.DeviceIdType.MESH
F32 = jnp.float32
BF16 = jnp.bfloat16

REGIONS = (
    (-1, 0, 0, 48),
    (1, 0, 48, 48),
    (0, -1, 96, 48),
    (0, 1, 144, 48),
    (-1, -1, 192, 16),
    (-1, 1, 208, 16),
    (1, -1, 224, 16),
    (1, 1, 240, 16),
)


def face_tables():
    source = np.full(FACE, -1, np.int64)
    table = np.zeros((8, FACE), np.int32)
    table[1] = DEAD
    for sx, sy, start, _ in REGIONS:
        xs = range(4) if sx == 0 else ((3,) if sx < 0 else (0,))
        ys = range(4) if sy == 0 else ((3,) if sy < 0 else (0,))
        row = start
        for slot in range(SLOTS):
            for vx in xs:
                for vy in ys:
                    for vz in range(4):
                        source[row] = slot * 64 + vx * 16 + vy * 4 + vz
                        table[0, row] = slot
                        table[1, row] = (
                            (8 * sx + vx + 1) * 4096 + (8 * sy + vy + 1) * 64 + vz + 1
                        )
                        row += 1
        table[2, start : start + (48 if sx * sy == 0 else 16)] = -sx
        table[3, start : start + (48 if sx * sy == 0 else 16)] = -sy
    for index, (_, _, start, count) in enumerate(REGIONS):
        table[4, start : start + count] = index
    pick = (source[:, None] == np.arange(ROWS)[None, :]).astype(np.float32)
    return pick, table


def block_codes(coords_ref, counts_ref):
    codes = []
    for slot in range(SLOTS):
        p = coords_ref[0, slot]
        code = (p // 16) * (4 * 4096) + ((p // 8) % 2) * (4 * 64) + (p % 8) * 4
        codes.append((code, slot < counts_ref[0, 0]))
    return codes


def by_slot(slot, codes):
    values = [jnp.where(live, code, DEAD) for code, live in codes]
    return jnp.where(slot == 0, values[0], jnp.where(slot == 1, values[1], values[2]))


def swap_faces(packed, landed, send_sems, recv_sems, extra=()):
    nx, ny = lax.axis_size("gx"), lax.axis_size("gy")
    gx, gy = lax.axis_index("gx"), lax.axis_index("gy")
    copies = []
    for index, (sx, sy, start, count) in enumerate(REGIONS):
        peer = (lax.rem(gx - sx + nx, nx), lax.rem(gy - sy + ny, ny))
        copies.append(
            pltpu.make_async_remote_copy(
                src_ref=packed.at[:, pl.ds(start, count), :],
                dst_ref=landed.at[:, pl.ds(start, count), :],
                send_sem=send_sems.at[index],
                recv_sem=recv_sems.at[index],
                device_id=peer,
                device_id_type=MESH,
            )
        )
        for source, target, sends, recvs in extra:
            copies.append(
                pltpu.make_async_remote_copy(
                    src_ref=source,
                    dst_ref=target.at[index],
                    send_sem=sends.at[index],
                    recv_sem=recvs.at[index],
                    device_id=peer,
                    device_id_type=MESH,
                )
            )
    return copies


def around():
    nx, ny = lax.axis_size("gx"), lax.axis_size("gy")
    gx, gy = lax.axis_index("gx"), lax.axis_index("gy")
    return [
        (lax.rem(gx - sx + nx, nx), lax.rem(gy - sy + ny, ny)) for sx, sy, _, _ in REGIONS
    ]


def build_windows(first, second, code_ref, coords_ref, win_ref):
    row = lax.broadcasted_iota(jnp.int32, (96, DATA), 0)
    pattern = (row // 16) * 4096 + ((row // 4) % 4) * 64 + row % 4
    offset = jnp.broadcast_to(code_ref[0:1, :], (96, DATA)) - pattern
    both = jnp.concatenate([first, second], axis=1)
    starts = []
    for slot in range(SLOTS):
        p = coords_ref[0, slot]
        starts.append((p // 16) * (4 * 4096) + ((p // 8) % 2) * (4 * 64) + (p % 8) * 4)
    for shift in range(9):
        placing = jnp.concatenate(
            [
                jnp.where(
                    offset == starts[slot] + (shift // 3) * 64 + shift % 3, 1.0, 0.0
                ).astype(BF16)
                for slot in range(SLOTS)
            ],
            axis=0,
        )
        rows = jnp.dot(placing, both, preferred_element_type=F32).astype(BF16)
        win_ref[0, shift] = rows[:, :C].reshape(SLOTS, 6, 16, C)
        win_ref[1, shift] = rows[:, C:].reshape(SLOTS, 6, 16, C)


def tap_rows(win_ref, field, tap):
    return win_ref[field, tap % 9, :, tap // 9 : tap // 9 + 4].reshape(ROWS, C)


def conv(win_ref, field, weight_ref):
    total = jnp.zeros((ROWS, C), F32)
    for tap in range(27):
        total += jnp.dot(
            tap_rows(win_ref, field, tap),
            weight_ref[tap * C : (tap + 1) * C, :],
            preferred_element_type=F32,
        )
    return total


def conv_back(win_ref, field, weight_ref):
    total = jnp.zeros((ROWS, C), F32)
    for tap in range(27):
        total += lax.dot_general(
            tap_rows(win_ref, field, 26 - tap),
            weight_ref[tap * C : (tap + 1) * C, :],
            (((1,), (1,)), ((), ())),
            preferred_element_type=F32,
        )
    return total


def live_rows(counts_ref):
    return lax.broadcasted_iota(jnp.int32, (ROWS, C), 0) < counts_ref[0, 0] * 64


BLOCK = 216
TILES = 27
PACKED = 56


class Ring:
    def __init__(self, own, out, inbox, sends, recvs, me, right, left, place):
        self.own, self.out, self.inbox = own, out, inbox
        self.sends, self.recvs = sends, recvs
        self.me = place(me)
        self.to_right = place(lax.rem(me + 1, 4))
        self.to_left = place(lax.rem(me + 3, 4))
        across = place(lax.rem(me + 2, 4))
        self.half = own.shape[1] // 2
        self.plan = (
            (across, self.half, right),
            (across, 0, left),
            (self.to_right, 0, right),
            (self.to_left, self.half, left),
            (self.to_right, self.half, right),
            (self.to_left, 0, left),
        )

    def copy(self, index, piece):
        target, base, peer = self.plan[index]
        return pltpu.make_async_remote_copy(
            src_ref=self.out.at[target, base + piece],
            dst_ref=self.inbox.at[index, piece],
            send_sem=self.sends.at[index, piece],
            recv_sem=self.recvs.at[index, piece],
            device_id=peer,
            device_id_type=MESH,
        )

    def start(self, piece):
        for index in range(4):
            self.copy(index, piece).start()

    def relay(self, piece):
        for index in range(2):
            target, base, _ = self.plan[4 + index]
            self.copy(index, piece).wait_recv()
            total = self.own[target, base + piece] + self.inbox[index, piece].astype(F32)
            self.out[target, base + piece] = total.astype(BF16)
            self.copy(4 + index, piece).start()

    def arrive(self, piece):
        for index in range(2, 6):
            self.copy(index, piece).wait_recv()

    def total(self, piece, upper):
        first, second = (3, 4) if upper else (2, 5)
        mine = self.own[self.me, piece + self.half * upper]
        return mine + self.inbox[first, piece].astype(F32) + self.inbox[second, piece].astype(F32)

    def drain(self):
        for piece in range(self.half):
            for index in range(6):
                self.copy(index, piece).wait_send()


def ring_scratch(nz, rows):
    return [
        pltpu.VMEM((4, nz, rows, 128), F32),
        pltpu.VMEM((4, nz, rows, 128), BF16),
        pltpu.VMEM((6, nz // 2, rows, 128), BF16),
        pltpu.SemaphoreType.DMA((6, nz // 2)),
        pltpu.SemaphoreType.DMA((6, nz // 2)),
    ]


def reduce_scratch(nz):
    return (
        ring_scratch(nz, BLOCK) * 2
        + ring_scratch(nz, PACKED) * 2
        + [
            pltpu.VMEM((2, nz, PACKED, 128), F32),
            pltpu.VMEM((2, nz, PACKED, 128), F32),
            pltpu.VMEM((2, PACKED, 128), F32),
            pltpu.VMEM((PACKED, 128), F32),
            pltpu.SemaphoreType.DMA((2, nz)),
            pltpu.SemaphoreType.DMA((2, nz)),
            pltpu.SemaphoreType.DMA((2,)),
        ]
    )


def swapped(t):
    return lax.rem(t, 2) * 2 + t // 2


def straight(t):
    return t


def chip_place():
    gx, gy = lax.axis_index("gx"), lax.axis_index("gy")
    z, x, core, y = gx // 4, (lax.rem(gx, 4) // 2) * 2 + lax.rem(gy, 2), lax.rem(gx, 2), gy // 2
    return x, y, z, core


def device_at(x, y, z, core):
    return (z * 4 + (x // 2) * 2 + core, y * 2 + lax.rem(x, 2))


def reduce_peers(nz):
    x, y, z, core = chip_place()
    return (
        [device_at(x, y, z, 1 - core)]
        + [device_at(lax.rem(x + step, 4), y, z, core) for step in (1, 3)]
        + [device_at(x, lax.rem(y + step, 4), z, core) for step in (1, 3)]
        + [device_at(x, y, lax.rem(z + step, nz), core) for step in range(1, nz)]
    )


def spread(rows, own, out, z):
    lane = lax.broadcasted_iota(jnp.int32, (8, 128), 1) // 32
    tiles = rows.reshape(TILES, 8, 128)
    for target in range(4):
        packed = []
        for group in range(7):
            tile = None
            for part in range(4):
                index = 4 * group + part
                if index >= TILES:
                    continue
                shift = (part - target) % 4 * 32
                moved = pltpu.roll(tiles[index], shift, 1) if shift else tiles[index]
                tile = moved if tile is None else jnp.where(lane == part, moved, tile)
            packed.append(tile)
        block = jnp.concatenate(packed, axis=0)
        own[target, z] = block
        out[target, z] = block.astype(BF16)


def unspread(packed):
    tiles = packed.reshape(7, 8, 128)
    rows = []
    for index in range(TILES):
        part = index % 4
        tile = tiles[index // 4]
        rows.append(pltpu.roll(tile, 128 - 32 * part, 1) if part else tile)
    rows += [jnp.zeros((8, 128), F32)] * (32 - TILES)
    return jnp.concatenate(rows, axis=0).T[:32, :BLOCK]


class Reduce:
    def __init__(self, nz, scale, term, scratch):
        self.nz, self.scale, self.term, self.half = nz, scale, term, nz // 2
        self.clock = 0
        self.x, self.y, self.z, self.core = chip_place()
        x, y, z, core = self.x, self.y, self.z, self.core
        xs, ys, ys2, xs2 = (scratch[5 * i : 5 * i + 5] for i in range(4))
        self.zown, self.zin, self.last, self.got, self.zsend, self.zrecv, self.psem = scratch[20:]
        x_right = device_at(lax.rem(x + 1, 4), y, z, core)
        x_left = device_at(lax.rem(x + 3, 4), y, z, core)
        y_right = device_at(x, lax.rem(y + 1, 4), z, core)
        y_left = device_at(x, lax.rem(y + 3, 4), z, core)
        self.firsts = [
            Ring(*xs, x, x_right, x_left, straight),
            Ring(*ys, y, y_right, y_left, straight),
        ]
        self.seconds = [
            Ring(*ys2, y, y_right, y_left, swapped),
            Ring(*xs2, x, x_right, x_left, straight),
        ]

    def advance(self):
        for stage, step in enumerate((self.relay, self.turn, self.turn_relay, self.along)):
            piece = self.clock - 1 - stage
            if 0 <= piece < self.half:
                step(piece)
        self.clock += 1
        return self.clock <= self.half + 4

    def begin(self, piece):
        term = self.term
        lane = lax.broadcasted_iota(jnp.int32, (BLOCK, 128), 1)
        even = (lane // 32) % 2 == 0
        below = lane < 64

        def place(ring, target, z, value):
            ring.own[target, z] = value
            ring.out[target, z] = value.astype(BF16)

        ring = self.firsts[0]
        for z in (piece, piece + self.half):
            for half in range(2):
                start = (4 * z + 2 * half) * BLOCK
                left, right = (
                    term[start : start + BLOCK, :128],
                    term[start : start + BLOCK, 128:],
                )
                place(ring, 2 * half, z, jnp.where(even, left, pltpu.roll(right, 32, 1)))
                place(ring, 2 * half + 1, z, jnp.where(even, pltpu.roll(left, 96, 1), right))
        ring.start(piece)
        ring = self.firsts[1]
        for z in (piece, piece + self.half):
            for pair in range(2):
                zero, one = (
                    term[start : start + BLOCK, 128 * pair : 128 * pair + 128]
                    for start in ((4 * z + 1) * BLOCK, (4 * z + 3) * BLOCK)
                )
                place(ring, 2 * pair, z, jnp.where(below, zero, pltpu.roll(one, 64, 1)))
                place(ring, 2 * pair + 1, z, jnp.where(below, pltpu.roll(zero, 64, 1), one))
        ring.start(piece)

    def relay(self, piece):
        for ring in self.firsts:
            ring.relay(piece)

    def turn(self, piece):
        for ring, following in zip(self.firsts, self.seconds):
            ring.arrive(piece)
            for upper in range(2):
                spread(
                    ring.total(piece, upper),
                    following.own,
                    following.out,
                    piece + upper * self.half,
                )
            following.start(piece)

    def turn_relay(self, piece):
        for ring in self.seconds:
            ring.relay(piece)

    def zcopy(self, color, to_z, slot):
        return pltpu.make_async_remote_copy(
            src_ref=self.zown.at[color, to_z],
            dst_ref=self.zin.at[color, slot],
            send_sem=self.zsend.at[color, to_z],
            recv_sem=self.zrecv.at[color, slot],
            device_id=device_at(self.x, self.y, to_z, self.core),
            device_id_type=MESH,
        )

    def along(self, piece):
        for color, ring in enumerate(self.seconds):
            ring.arrive(piece)
            for upper in range(2):
                to_z = piece + upper * self.half
                self.zown[color, to_z] = ring.total(piece, upper)

                @pl.when(self.z != to_z)
                def _():
                    self.zcopy(color, to_z, self.z).start()

    def finish(self, first_ref, second_ref):
        for color in range(2):
            self.last[color] = self.zown[color, self.z]
            for from_z in range(self.nz):

                @pl.when(self.z != from_z)
                def _():
                    self.zcopy(color, from_z, from_z).wait_recv()
                    self.last[color] += self.zin[color, from_z]

        copy = pltpu.make_async_remote_copy(
            src_ref=self.last.at[1 - self.core],
            dst_ref=self.got,
            send_sem=self.psem.at[0],
            recv_sem=self.psem.at[1],
            device_id=device_at(self.x, self.y, self.z, 1 - self.core),
            device_id_type=MESH,
        )
        copy.start()
        for ring in self.firsts + self.seconds:
            ring.drain()
        for color in range(2):
            for to_z in range(self.nz):

                @pl.when(self.z != to_z)
                def _():
                    self.zcopy(color, to_z, self.z).wait_send()

        copy.wait()
        mine, other = self.last[self.core] * self.scale, self.got[...] * self.scale
        first = self.core == 0
        first_ref[...] = unspread(jnp.where(first, mine, other))
        second_ref[...] = unspread(jnp.where(first, other, mine))


def gradient_taps(piece, nz):
    needed = []
    for index in range(piece + 1):
        taps = set()
        for z in (index, index + nz // 2):
            taps |= set(range(864 * z // C, -(-864 * (z + 1) // C)))
        needed.append(taps)
    return sorted(needed[-1].difference(*needed[:-1]))


def runs(taps):
    out = []
    for tap in taps:
        if out and out[-1][1] == tap:
            out[-1][1] = tap + 1
        else:
            out.append([tap, tap + 1])
    return out


def step_kernel(
    nz,
    scale,
    feat_hbm,
    cot_hbm,
    pick_hbm,
    table_hbm,
    coords_ref,
    counts_ref,
    w1_hbm,
    w2_hbm,
    out_hbm,
    grad_hbm,
    first_hbm,
    second_hbm,
    out_ref,
    grad_ref,
    first_ref,
    second_ref,
    put_sems,
    feat,
    cot,
    pick,
    table,
    w1,
    w2,
    load_sems,
    packed,
    landed,
    send_sems,
    recv_sems,
    sent_code,
    codes_in,
    code_send,
    code_recv,
    code,
    win,
    rows,
    pair_win,
    pair_rows,
    pair_sems,
    turned,
    term,
    *scratch,
):
    nx, ny = lax.axis_size("gx"), lax.axis_size("gy")
    gx, gy = lax.axis_index("gx"), lax.axis_index("gy")
    x, y, z, core = chip_place()
    peers = around() + reduce_peers(nz)
    barrier = pltpu.get_barrier_semaphore()
    for peer in peers:
        pl.semaphore_signal(barrier, inc=1, device_id=peer, device_id_type=MESH)
    loads = [
        pltpu.make_async_copy(source, target, load_sems.at[index])
        for index, (source, target) in enumerate(
            (
                (feat_hbm, feat),
                (cot_hbm, cot),
                (pick_hbm, pick),
                (table_hbm, table),
                (w1_hbm, w1),
                (w2_hbm, w2),
            )
        )
    ]
    for load in loads:
        load.start()
    for load in loads[:4]:
        load.wait()
    blocks = block_codes(coords_ref, counts_ref)
    to_x = gx + table[2:3, :]
    to_y = gy + table[3:4, :]
    inside = (to_x >= 0) & (to_x < nx) & (to_y >= 0) & (to_y < ny)
    sent = table[1:2, :] + by_slot(table[0:1, :], blocks)
    sent_code[...] = jnp.broadcast_to(jnp.where(inside, sent, DEAD), (8, FACE))
    packed[0, 0] = jnp.dot(pick[...], feat[...], preferred_element_type=F32).astype(BF16)
    packed[0, 1] = jnp.dot(pick[...], cot[...], preferred_element_type=F32).astype(BF16)
    pl.semaphore_wait(barrier, len(peers))
    faces = swap_faces(
        packed.at[0],
        landed.at[0],
        send_sems.at[0],
        recv_sems.at[0],
        ((sent_code, codes_in, code_send, code_recv),),
    )
    for copy in faces:
        copy.start()
    lane = lax.broadcasted_iota(jnp.int32, (8, ROWS), 1)
    voxel = lane % 64
    own = (voxel // 16 + 1) * 4096 + ((voxel // 4) % 4 + 1) * 64 + voxel % 4 + 1
    code[:, FACE:] = own + by_slot(lane // 64, blocks)
    live = live_rows(counts_ref)
    region = jnp.broadcast_to(table[4:5, :], (8, FACE))
    for copy in faces:
        copy.wait_recv()
    got = codes_in[0]
    for index in range(1, 8):
        got = jnp.where(region == index, codes_in[index], got)
    code[:, :FACE] = got
    build_windows(
        jnp.concatenate([landed[0, 0], feat[...]], axis=0),
        jnp.concatenate([landed[0, 1], cot[...]], axis=0),
        code,
        coords_ref,
        win.at[0],
    )
    pair = [
        pltpu.make_async_remote_copy(
            src_ref=source,
            dst_ref=target,
            send_sem=pair_sems.at[2 * index],
            recv_sem=pair_sems.at[2 * index + 1],
            device_id=device_at(x, y, z, 1 - core),
            device_id_type=MESH,
        )
        for index, (source, target) in enumerate(
            ((win.at[0, 1 - core], pair_win), (rows.at[core], pair_rows))
        )
    ]
    pair[0].start()
    loads[4].wait()
    pre = conv(win.at[0], 0, w1)
    gate = jax.nn.sigmoid(pre)
    hidden = jnp.where(live, pre * gate, 0.0).astype(BF16)
    rows[0] = hidden
    packed[1, 0] = jnp.dot(pick[...], hidden, preferred_element_type=F32).astype(BF16)
    loads[5].wait()
    hidden_grad = conv_back(win.at[0], 1, w2)
    pre_grad = jnp.where(live, hidden_grad * gate * (1.0 + pre * (1.0 - gate)), 0.0).astype(BF16)
    rows[1] = pre_grad
    packed[1, 1] = jnp.dot(pick[...], pre_grad, preferred_element_type=F32).astype(BF16)
    pair[1].start()
    more_faces = swap_faces(
        packed.at[1], landed.at[1], send_sems.at[1], recv_sems.at[1]
    )
    for copy in more_faces:
        copy.start()
    for copy in pair:
        copy.wait_recv()

    def window(tap):
        shift, start = lax.rem(tap, 9), tap // 9
        return jnp.concatenate(
            [
                win[0, core, shift, :, pl.ds(start, 4)].reshape(ROWS, C),
                pair_win[shift, :, pl.ds(start, 4)].reshape(ROWS, C),
            ],
            axis=0,
        )

    both = jnp.concatenate([rows[1 - core], pair_rows[...]], axis=0)
    turned[...] = both.astype(F32).T.astype(BF16)
    reduce = Reduce(nz, scale, term, scratch)
    for piece in range(nz // 2):
        for start, stop in runs(gradient_taps(piece, nz)):

            @pl.when(core == 0)
            def _():
                @pl.loop(start, stop)
                def _(tap):
                    term[pl.ds(pl.multiple_of(tap * C, C), C), :] = lax.dot_general(
                        window(tap),
                        jnp.concatenate([rows[1], pair_rows[...]], axis=0),
                        (((0,), (0,)), ((), ())),
                        preferred_element_type=F32,
                    )

            @pl.when(core == 1)
            def _():
                @pl.loop(start, stop)
                def _(tap):
                    term[pl.ds(pl.multiple_of(tap * C, C), C), :] = jnp.dot(
                        turned[...], window(26 - tap), preferred_element_type=F32
                    )

        reduce.begin(piece)
        reduce.advance()
    for copy in more_faces:
        copy.wait_recv()
    build_windows(
        jnp.concatenate([landed[1, 0], rows[0]], axis=0),
        jnp.concatenate([landed[1, 1], rows[1]], axis=0),
        code,
        coords_ref,
        win.at[1],
    )
    reduce.advance()
    out_ref[...] = jnp.where(live, conv(win.at[1], 0, w2), 0.0)
    puts = [
        pltpu.make_async_copy(source, target, put_sems.at[index])
        for index, (source, target) in enumerate(
            (
                (out_ref, out_hbm),
                (grad_ref, grad_hbm),
                (first_ref, first_hbm),
                (second_ref, second_hbm),
            )
        )
    ]
    puts[0].start()
    reduce.advance()
    grad_ref[...] = jnp.where(live, conv_back(win.at[1], 1, w1), 0.0)
    puts[1].start()
    while reduce.advance():
        pass
    for copy in faces + more_faces + pair:
        copy.wait_send()
    reduce.finish(first_ref, second_ref)
    for put in puts[2:]:
        put.start()
    for put in puts:
        put.wait()


def store_kernel(*refs):
    sources, targets, held, sems = refs[:4], refs[4:8], refs[8:12], refs[12]
    takes = [
        pltpu.make_async_copy(sources[index], held[index], sems.at[index]) for index in range(4)
    ]
    puts = [
        pltpu.make_async_copy(held[index], targets[index], sems.at[4 + index])
        for index in range(4)
    ]
    for take in takes:
        take.start()
    for take, put in zip(takes, puts):
        take.wait()
        put.start()
    for put in puts:
        put.wait()


def vmem():
    return pl.BlockSpec(memory_space=pltpu.VMEM)


def smem():
    return pl.BlockSpec(memory_space=pltpu.SMEM)


def hbm():
    return pl.BlockSpec(memory_space=pltpu.HBM)


def per_device(features, block_coords, block_counts, first_weight, second_weight, cotangent):
    feat = features.reshape(ROWS, C)
    cot = cotangent.reshape(ROWS, C)
    coords = block_coords.reshape(1, SLOTS)
    counts = block_counts.reshape(1, 1)
    pick_np, table_np = face_tables()
    pick = jnp.asarray(pick_np, BF16)
    table = jnp.asarray(table_np)
    struct = jax.ShapeDtypeStruct
    scale = 1.0 / math.sqrt(64 * SLOTS * lax.axis_size("gx") * lax.axis_size("gy"))
    nz = lax.axis_size("gx") // 4
    window = (9, SLOTS, 6, 16, C)
    dma = pltpu.SemaphoreType.DMA
    out, grad, first_grad, second_grad = pl.pallas_call(
        functools.partial(step_kernel, nz, scale),
        out_shape=(
            struct((ROWS, C), F32),
            struct((ROWS, C), F32),
            struct((32, BLOCK), F32),
            struct((32, BLOCK), F32),
        ),
        in_specs=[hbm()] * 4 + [smem()] * 2 + [hbm()] * 2,
        out_specs=(hbm(),) * 4,
        scratch_shapes=[
            pltpu.VMEM((ROWS, C), F32),
            pltpu.VMEM((ROWS, C), F32),
            pltpu.VMEM((32, BLOCK), F32),
            pltpu.VMEM((32, BLOCK), F32),
            dma((4,)),
            pltpu.VMEM((ROWS, C), BF16),
            pltpu.VMEM((ROWS, C), BF16),
            pltpu.VMEM((FACE, ROWS), BF16),
            pltpu.VMEM((8, FACE), jnp.int32),
            pltpu.VMEM((27 * C, C), BF16),
            pltpu.VMEM((27 * C, C), BF16),
            dma((6,)),
            pltpu.VMEM((2, 2, FACE, C), BF16),
            pltpu.VMEM((2, 2, FACE, C), BF16),
            dma((2, 8)),
            dma((2, 8)),
            pltpu.VMEM((8, FACE), jnp.int32),
            pltpu.VMEM((8, 8, FACE), jnp.int32),
            dma((8,)),
            dma((8,)),
            pltpu.VMEM((8, DATA), jnp.int32),
            pltpu.VMEM((2, 2) + window, BF16),
            pltpu.VMEM((2, ROWS, C), BF16),
            pltpu.VMEM(window, BF16),
            pltpu.VMEM((ROWS, C), BF16),
            dma((4,)),
            pltpu.VMEM((C, 2 * ROWS), BF16),
            pltpu.VMEM((27 * C, C), F32),
        ]
        + reduce_scratch(nz),
        compiler_params=pltpu.CompilerParams(
            collective_id=0, has_side_effects=True, vmem_limit_bytes=LIMIT
        ),
        name="step",
    )(feat, cot, pick, table, coords, counts, first_weight, second_weight)
    results = (out, grad, first_grad, second_grad)
    out, grad, first_grad, second_grad = pl.pallas_call(
        store_kernel,
        out_shape=[struct(result.shape, F32) for result in results],
        in_specs=[hbm()] * 4,
        out_specs=[hbm()] * 4,
        scratch_shapes=[pltpu.VMEM(result.shape, F32) for result in results] + [dma((8,))],
        name="store",
    )(*results)
    return out.reshape(features.shape), grad.reshape(features.shape), first_grad.T, second_grad.T


def solution(mesh):
    placed = (
        P("gx", "gy", None, None, None),
        P("gx", "gy", None),
        P("gx", "gy"),
        P(),
        P(),
        P("gx", "gy", None, None, None),
    )
    return jax.shard_map(
        per_device,
        mesh=mesh,
        in_specs=placed,
        out_specs=(
            P("gx", "gy", None, None, None),
            P("gx", "gy", None, None, None),
            P("gx", "gy"),
            P("gx", "gy"),
        ),
        check_vma=False,
    )
```

profile of v0, /device:TPU:97, one launch (start us, length us, event | category | flops | bytes accessed | tf_op | source)
XLA Modules:
  0.0 64.5 jit_solution(16939758810077501337)
XLA Ops:
  1.3 61.3 %step.1 = (f32[192,256]{1,0:T(8,128)}, f32[192,256]{1,0:T(8,128)}, f32[32,216]{1,0:T(8,128)}, f32[32,216]{1,0:T(8,128)}) custom-call(bf16[192,256]{1,0:T(8,128)(2,1)} %bitcast.7, bf16[192,256]{1,0:T(8,128)(2,1)} %bitcast.8, bf16[256,192]{1,0:T(8,128)(2,1)} %constant.4.clone.pick_hbm, s32[8,256]{1,0:T(8,128)} %constant.5.clone.table_hbm, s32[1,3]{1,0:T(1,128)} %bitcast.9, ...), custom_call_target="tpu_custom_call" | custom-call | tf_op jit(solution)/shard_map/step/pallas_call | solution.py:728
  62.6 1.8 %store.1 = (f32[192,256]{1,0:T(8,128)}, f32[192,256]{1,0:T(8,128)}, f32[32,216]{1,0:T(8,128)}, f32[32,216]{1,0:T(8,128)}) custom-call(f32[192,256]{1,0:T(8,128)} %get-tuple-element.12.refs_0_, f32[192,256]{1,0:T(8,128)} %get-tuple-element.13.refs_1_, f32[32,216]{1,0:T(8,128)} %get-tuple-element.14.refs_2_, f32[32,216]{1,0:T(8,128)} %get-tuple-element.15.refs_3_), custom_call_target="tpu_custom_call" | custom-call | tf_op jit(solution)/shard_map/store/pallas_call | solution.py:775
where the time goes:
time: 64.6 us; the launch traced here: 64.5 us
  Pallas kernels  63.1 us (98%)
  between operations  1.45 us (2%)
    pallas_call x1, Pallas kernels, per_device(): pl.pallas_call(functools.partial(step_kernel, nz, scale), out_shape=(stru...  61.3 us
    pallas_call x1, Pallas kernels, per_device(): pl.pallas_call(store_kernel, out_shape=[struct(result.shape, F32) for res...  1.78 us

commit v1 on v0

--- a/solution.py
+++ b/solution.py
@@ -15,7 +15,7 @@
 FACE = 256
 DATA = FACE + ROWS
 DEAD = -(1 << 24)
-LIMIT = 56 << 20
+LIMIT = 58 << 20
 MESH = pl.DeviceIdType.MESH
 F32 = jnp.float32
 BF16 = jnp.bfloat16
@@ -72,33 +72,20 @@
     return jnp.where(slot == 0, values[0], jnp.where(slot == 1, values[1], values[2]))
 
 
-def swap_faces(packed, landed, send_sems, recv_sems, extra=()):
-    nx, ny = lax.axis_size("gx"), lax.axis_size("gy")
-    gx, gy = lax.axis_index("gx"), lax.axis_index("gy")
+def swap_faces(packed, landed, send_sems, recv_sems, index_last=False):
     copies = []
-    for index, (sx, sy, start, count) in enumerate(REGIONS):
-        peer = (lax.rem(gx - sx + nx, nx), lax.rem(gy - sy + ny, ny))
+    for index, (peer, (_, _, start, count)) in enumerate(zip(around(), REGIONS)):
+        part = pl.ds(start, count)
         copies.append(
             pltpu.make_async_remote_copy(
-                src_ref=packed.at[:, pl.ds(start, count), :],
-                dst_ref=landed.at[:, pl.ds(start, count), :],
+                src_ref=packed if index_last else packed.at[part],
+                dst_ref=landed.at[index] if index_last else landed.at[part],
                 send_sem=send_sems.at[index],
                 recv_sem=recv_sems.at[index],
                 device_id=peer,
                 device_id_type=MESH,
             )
         )
-        for source, target, sends, recvs in extra:
-            copies.append(
-                pltpu.make_async_remote_copy(
-                    src_ref=source,
-                    dst_ref=target.at[index],
-                    send_sem=sends.at[index],
-                    recv_sem=recvs.at[index],
-                    device_id=peer,
-                    device_id_type=MESH,
-                )
-            )
     return copies
 
 
@@ -110,50 +97,46 @@
     ]
 
 
-def build_windows(first, second, code_ref, coords_ref, win_ref):
+def build_placing(code, coords_ref, placing):
     row = lax.broadcasted_iota(jnp.int32, (96, DATA), 0)
     pattern = (row // 16) * 4096 + ((row // 4) % 4) * 64 + row % 4
-    offset = jnp.broadcast_to(code_ref[0:1, :], (96, DATA)) - pattern
-    both = jnp.concatenate([first, second], axis=1)
-    starts = []
+    offset = jnp.broadcast_to(code, (96, DATA)) - pattern
     for slot in range(SLOTS):
         p = coords_ref[0, slot]
-        starts.append((p // 16) * (4 * 4096) + ((p // 8) % 2) * (4 * 64) + (p % 8) * 4)
+        start = (p // 16) * (4 * 4096) + ((p // 8) % 2) * (4 * 64) + (p % 8) * 4
+        for shift in range(9):
+            placing[shift, slot * 96 : slot * 96 + 96, :] = jnp.where(
+                offset == start + (shift // 3) * 64 + shift % 3, 1.0, 0.0
+            ).astype(BF16)
+
+
+def build_windows(landed, own, placing, win_ref):
+    data = jnp.concatenate([landed, own], axis=0)
     for shift in range(9):
-        placing = jnp.concatenate(
-            [
-                jnp.where(
-                    offset == starts[slot] + (shift // 3) * 64 + shift % 3, 1.0, 0.0
-                ).astype(BF16)
-                for slot in range(SLOTS)
-            ],
-            axis=0,
-        )
-        rows = jnp.dot(placing, both, preferred_element_type=F32).astype(BF16)
-        win_ref[0, shift] = rows[:, :C].reshape(SLOTS, 6, 16, C)
-        win_ref[1, shift] = rows[:, C:].reshape(SLOTS, 6, 16, C)
-
-
-def tap_rows(win_ref, field, tap):
-    return win_ref[field, tap % 9, :, tap // 9 : tap // 9 + 4].reshape(ROWS, C)
-
-
-def conv(win_ref, field, weight_ref):
+        rows = jnp.dot(placing[shift], data, preferred_element_type=F32).astype(BF16)
+        win_ref[shift] = rows.reshape(SLOTS, 6, 16, C)
+
+
+def tap_rows(win_ref, tap):
+    return win_ref[tap % 9, :, tap // 9 : tap // 9 + 4].reshape(ROWS, C)
+
+
+def conv(win_ref, weight_ref):
     total = jnp.zeros((ROWS, C), F32)
     for tap in range(27):
         total += jnp.dot(
-            tap_rows(win_ref, field, tap),
+            tap_rows(win_ref, tap),
             weight_ref[tap * C : (tap + 1) * C, :],
             preferred_element_type=F32,
         )
     return total
 
 
-def conv_back(win_ref, field, weight_ref):
+def conv_back(win_ref, weight_ref):
     total = jnp.zeros((ROWS, C), F32)
     for tap in range(27):
         total += lax.dot_general(
-            tap_rows(win_ref, field, 26 - tap),
+            tap_rows(win_ref, 26 - tap),
             weight_ref[tap * C : (tap + 1) * C, :],
             (((1,), (1,)), ((), ())),
             preferred_element_type=F32,
@@ -243,11 +226,11 @@
         + [
             pltpu.VMEM((2, nz, PACKED, 128), F32),
             pltpu.VMEM((2, nz, PACKED, 128), F32),
+            pltpu.VMEM((2, nz, PACKED, 128), BF16),
+            pltpu.VMEM((2, nz, PACKED, 128), BF16),
             pltpu.VMEM((2, PACKED, 128), F32),
-            pltpu.VMEM((PACKED, 128), F32),
             pltpu.SemaphoreType.DMA((2, nz)),
             pltpu.SemaphoreType.DMA((2, nz)),
-            pltpu.SemaphoreType.DMA((2,)),
         ]
     )
 
@@ -276,7 +259,7 @@
         [device_at(x, y, z, 1 - core)]
         + [device_at(lax.rem(x + step, 4), y, z, core) for step in (1, 3)]
         + [device_at(x, lax.rem(y + step, 4), z, core) for step in (1, 3)]
-        + [device_at(x, y, lax.rem(z + step, nz), core) for step in range(1, nz)]
+        + [device_at(x, y, lax.rem(z + step, nz), c) for step in range(1, nz) for c in range(2)]
     )
 
 
@@ -318,7 +301,7 @@
         self.x, self.y, self.z, self.core = chip_place()
         x, y, z, core = self.x, self.y, self.z, self.core
         xs, ys, ys2, xs2 = (scratch[5 * i : 5 * i + 5] for i in range(4))
-        self.zown, self.zin, self.last, self.got, self.zsend, self.zrecv, self.psem = scratch[20:]
+        self.zown, self.zin, self.zout, self.zlate, self.last, self.zsend, self.zrecv = scratch[20:]
         x_right = device_at(lax.rem(x + 1, 4), y, z, core)
         x_left = device_at(lax.rem(x + 3, 4), y, z, core)
         y_right = device_at(x, lax.rem(y + 1, 4), z, core)
@@ -392,13 +375,14 @@
         for ring in self.seconds:
             ring.relay(piece)
 
-    def zcopy(self, color, to_z, slot):
+    def zcopy(self, color, to_z, source, slot):
+        late = to_z % self.half == self.half - 1
         return pltpu.make_async_remote_copy(
-            src_ref=self.zown.at[color, to_z],
-            dst_ref=self.zin.at[color, slot],
+            src_ref=(self.zout if late else self.zown).at[color, to_z],
+            dst_ref=(self.zlate if late else self.zin).at[source, slot],
             send_sem=self.zsend.at[color, to_z],
-            recv_sem=self.zrecv.at[color, slot],
-            device_id=device_at(self.x, self.y, to_z, self.core),
+            recv_sem=self.zrecv.at[source, slot],
+            device_id=device_at(self.x, self.y, to_z, color),
             device_id_type=MESH,
         )
 
@@ -407,45 +391,50 @@
             ring.arrive(piece)
             for upper in range(2):
                 to_z = piece + upper * self.half
-                self.zown[color, to_z] = ring.total(piece, upper)
-
-                @pl.when(self.z != to_z)
+                total = ring.total(piece, upper)
+                self.zown[color, to_z] = total
+                if piece == self.half - 1:
+                    self.zout[color, to_z] = total.astype(BF16)
+
+                @pl.when((self.z != to_z) | (self.core != color))
                 def _():
-                    self.zcopy(color, to_z, self.z).start()
+                    self.zcopy(color, to_z, self.core, self.z).start()
+
+    def gather(self, late):
+        inbox, to_z = (self.zlate, self.half - 1) if late else (self.zin, 0)
+        for source in range(2):
+            for from_z in range(self.nz):
+
+                @pl.when((self.z != from_z) | (self.core != source))
+                def _():
+                    self.zcopy(0, to_z, source, from_z).wait_recv()
+                    self.last[source] += inbox[source, from_z].astype(F32)
 
     def finish(self, first_ref, second_ref):
-        for color in range(2):
-            self.last[color] = self.zown[color, self.z]
-            for from_z in range(self.nz):
-
-                @pl.when(self.z != from_z)
-                def _():
-                    self.zcopy(color, from_z, from_z).wait_recv()
-                    self.last[color] += self.zin[color, from_z]
-
-        copy = pltpu.make_async_remote_copy(
-            src_ref=self.last.at[1 - self.core],
-            dst_ref=self.got,
-            send_sem=self.psem.at[0],
-            recv_sem=self.psem.at[1],
-            device_id=device_at(self.x, self.y, self.z, 1 - self.core),
-            device_id_type=MESH,
-        )
-        copy.start()
+        self.last[self.core] = self.zown[self.core, self.z]
+        self.last[1 - self.core] = jnp.zeros((PACKED, 128), F32)
+        late = lax.rem(self.z, self.half) == self.half - 1
+
+        @pl.when(late)
+        def _():
+            self.gather(True)
+
+        @pl.when(jnp.logical_not(late))
+        def _():
+            self.gather(False)
+
+        first_ref[...] = unspread(self.last[0] * self.scale)
+        second_ref[...] = unspread(self.last[1] * self.scale)
+
+    def drain(self):
         for ring in self.firsts + self.seconds:
             ring.drain()
         for color in range(2):
             for to_z in range(self.nz):
 
-                @pl.when(self.z != to_z)
+                @pl.when((self.z != to_z) | (self.core != color))
                 def _():
-                    self.zcopy(color, to_z, self.z).wait_send()
-
-        copy.wait()
-        mine, other = self.last[self.core] * self.scale, self.got[...] * self.scale
-        first = self.core == 0
-        first_ref[...] = unspread(jnp.where(first, mine, other))
-        second_ref[...] = unspread(jnp.where(first, other, mine))
+                    self.zcopy(color, to_z, self.core, self.z).wait_send()
 
 
 def gradient_taps(piece, nz):
@@ -503,7 +492,7 @@
     codes_in,
     code_send,
     code_recv,
-    code,
+    placing,
     win,
     rows,
     pair_win,
@@ -545,35 +534,36 @@
     sent_code[...] = jnp.broadcast_to(jnp.where(inside, sent, DEAD), (8, FACE))
     packed[0, 0] = jnp.dot(pick[...], feat[...], preferred_element_type=F32).astype(BF16)
     packed[0, 1] = jnp.dot(pick[...], cot[...], preferred_element_type=F32).astype(BF16)
+    faces = [
+        swap_faces(
+            packed.at[phase, field],
+            landed.at[phase, field],
+            send_sems.at[phase, field],
+            recv_sems.at[phase, field],
+        )
+        for phase in range(2)
+        for field in range(2)
+    ]
+    code_copies = swap_faces(sent_code, codes_in, code_send, code_recv, True)
     pl.semaphore_wait(barrier, len(peers))
-    faces = swap_faces(
-        packed.at[0],
-        landed.at[0],
-        send_sems.at[0],
-        recv_sems.at[0],
-        ((sent_code, codes_in, code_send, code_recv),),
-    )
-    for copy in faces:
+    for copy in code_copies + faces[0] + faces[1]:
         copy.start()
     lane = lax.broadcasted_iota(jnp.int32, (8, ROWS), 1)
     voxel = lane % 64
     own = (voxel // 16 + 1) * 4096 + ((voxel // 4) % 4 + 1) * 64 + voxel % 4 + 1
-    code[:, FACE:] = own + by_slot(lane // 64, blocks)
+    own += by_slot(lane // 64, blocks)
     live = live_rows(counts_ref)
     region = jnp.broadcast_to(table[4:5, :], (8, FACE))
-    for copy in faces:
+    for copy in code_copies:
         copy.wait_recv()
     got = codes_in[0]
     for index in range(1, 8):
         got = jnp.where(region == index, codes_in[index], got)
-    code[:, :FACE] = got
-    build_windows(
-        jnp.concatenate([landed[0, 0], feat[...]], axis=0),
-        jnp.concatenate([landed[0, 1], cot[...]], axis=0),
-        code,
-        coords_ref,
-        win.at[0],
-    )
+    code = jnp.concatenate([got, own], axis=1)[0:1, :]
+    build_placing(code, coords_ref, placing)
+    for copy in faces[0]:
+        copy.wait_recv()
+    build_windows(landed[0, 0], feat[...], placing, win.at[0, 0])
     pair = [
         pltpu.make_async_remote_copy(
             src_ref=source,
@@ -587,23 +577,23 @@
             ((win.at[0, 1 - core], pair_win), (rows.at[core], pair_rows))
         )
     ]
-    pair[0].start()
     loads[4].wait()
-    pre = conv(win.at[0], 0, w1)
+    pre = conv(win.at[0, 0], w1)
     gate = jax.nn.sigmoid(pre)
     hidden = jnp.where(live, pre * gate, 0.0).astype(BF16)
     rows[0] = hidden
     packed[1, 0] = jnp.dot(pick[...], hidden, preferred_element_type=F32).astype(BF16)
+    for copy in faces[1]:
+        copy.wait_recv()
+    build_windows(landed[0, 1], cot[...], placing, win.at[0, 1])
+    pair[0].start()
     loads[5].wait()
-    hidden_grad = conv_back(win.at[0], 1, w2)
+    hidden_grad = conv_back(win.at[0, 1], w2)
     pre_grad = jnp.where(live, hidden_grad * gate * (1.0 + pre * (1.0 - gate)), 0.0).astype(BF16)
     rows[1] = pre_grad
     packed[1, 1] = jnp.dot(pick[...], pre_grad, preferred_element_type=F32).astype(BF16)
     pair[1].start()
-    more_faces = swap_faces(
-        packed.at[1], landed.at[1], send_sems.at[1], recv_sems.at[1]
-    )
-    for copy in more_faces:
+    for copy in faces[2] + faces[3]:
         copy.start()
     for copy in pair:
         copy.wait_recv()
@@ -645,17 +635,12 @@
 
         reduce.begin(piece)
         reduce.advance()
-    for copy in more_faces:
-        copy.wait_recv()
-    build_windows(
-        jnp.concatenate([landed[1, 0], rows[0]], axis=0),
-        jnp.concatenate([landed[1, 1], rows[1]], axis=0),
-        code,
-        coords_ref,
-        win.at[1],
-    )
+    for field in range(2):
+        for copy in faces[2 + field]:
+            copy.wait_recv()
+        build_windows(landed[1, field], rows[field], placing, win.at[1, field])
     reduce.advance()
-    out_ref[...] = jnp.where(live, conv(win.at[1], 0, w2), 0.0)
+    out_ref[...] = jnp.where(live, conv(win.at[1, 0], w2), 0.0)
     puts = [
         pltpu.make_async_copy(source, target, put_sems.at[index])
         for index, (source, target) in enumerate(
@@ -669,15 +654,16 @@
     ]
     puts[0].start()
     reduce.advance()
-    grad_ref[...] = jnp.where(live, conv_back(win.at[1], 1, w1), 0.0)
+    grad_ref[...] = jnp.where(live, conv_back(win.at[1, 1], w1), 0.0)
     puts[1].start()
     while reduce.advance():
         pass
-    for copy in faces + more_faces + pair:
-        copy.wait_send()
     reduce.finish(first_ref, second_ref)
     for put in puts[2:]:
         put.start()
+    for copy in code_copies + sum(faces, []) + pair:
+        copy.wait_send()
+    reduce.drain()
     for put in puts:
         put.wait()
 
@@ -750,13 +736,13 @@
             dma((6,)),
             pltpu.VMEM((2, 2, FACE, C), BF16),
             pltpu.VMEM((2, 2, FACE, C), BF16),
-            dma((2, 8)),
-            dma((2, 8)),
+            dma((2, 2, 8)),
+            dma((2, 2, 8)),
             pltpu.VMEM((8, FACE), jnp.int32),
             pltpu.VMEM((8, 8, FACE), jnp.int32),
             dma((8,)),
             dma((8,)),
-            pltpu.VMEM((8, DATA), jnp.int32),
+            pltpu.VMEM((9, 96 * SLOTS, DATA), BF16),
             pltpu.VMEM((2, 2) + window, BF16),
             pltpu.VMEM((2, ROWS, C), BF16),
             pltpu.VMEM(window, BF16),

time: 64.6 us -> 63.4 us (0.981)
  Pallas kernels: 63.1 us -> 61.9 us
    pallas_call x1, Pallas kernels: 61.3 us -> 60.1 us  [per_device(): pl.pallas_call(functools.partial(step_kernel, nz, scale), out_shape=(stru...]
where the time goes in v1:
time: 63.4 us; the launch traced here: 63.3 us
  Pallas kernels  61.9 us (98%)
  between operations  1.45 us (2%)
    pallas_call x1, Pallas kernels, per_device(): pl.pallas_call(functools.partial(step_kernel, nz, scale), out_shape=(stru...  60.1 us
    pallas_call x1, Pallas kernels, per_device(): pl.pallas_call(store_kernel, out_shape=[struct(result.shape, F32) for res...  1.78 us

profile of v1, /device:TPU:97, one launch (start us, length us, event | category | flops | bytes accessed | tf_op | source)
XLA Modules:
  0.0 63.3 jit_solution(1570906349200172400)
XLA Ops:
  1.3 60.1 %step.1 = (f32[192,256]{1,0:T(8,128)}, f32[192,256]{1,0:T(8,128)}, f32[32,216]{1,0:T(8,128)}, f32[32,216]{1,0:T(8,128)}) custom-call(bf16[192,256]{1,0:T(8,128)(2,1)} %bitcast.7, bf16[192,256]{1,0:T(8,128)(2,1)} %bitcast.8, bf16[256,192]{1,0:T(8,128)(2,1)} %constant.4.clone.pick_hbm, s32[8,256]{1,0:T(8,128)} %constant.5.clone.table_hbm, s32[1,3]{1,0:T(1,128)} %bitcast.9, ...), custom_call_target="tpu_custom_call" | custom-call | tf_op jit(solution)/shard_map/step/pallas_call | solution.py:714
  61.4 1.8 %store.1 = (f32[192,256]{1,0:T(8,128)}, f32[192,256]{1,0:T(8,128)}, f32[32,216]{1,0:T(8,128)}, f32[32,216]{1,0:T(8,128)}) custom-call(f32[192,256]{1,0:T(8,128)} %get-tuple-element.12.refs_0_, f32[192,256]{1,0:T(8,128)} %get-tuple-element.13.refs_1_, f32[32,216]{1,0:T(8,128)} %get-tuple-element.14.refs_2_, f32[32,216]{1,0:T(8,128)} %get-tuple-element.15.refs_3_), custom_call_target="tpu_custom_call" | custom-call | tf_op jit(solution)/shard_map/store/pallas_call | solution.py:761

commit v2 on v1

--- a/solution.py
+++ b/solution.py
@@ -12,7 +12,7 @@
 C = 256
 SLOTS = 3
 ROWS = 192
-FACE = 256
+FACE = 192
 DATA = FACE + ROWS
 DEAD = -(1 << 24)
 LIMIT = 58 << 20
@@ -21,40 +21,41 @@
 BF16 = jnp.bfloat16
 
 REGIONS = (
-    (-1, 0, 0, 48),
-    (1, 0, 48, 48),
-    (0, -1, 96, 48),
-    (0, 1, 144, 48),
-    (-1, -1, 192, 16),
-    (-1, 1, 208, 16),
-    (1, -1, 224, 16),
-    (1, 1, 240, 16),
+    (-1, 0, 0, 32),
+    (1, 0, 32, 32),
+    (0, -1, 64, 32),
+    (0, 1, 96, 32),
+    (-1, -1, 128, 16),
+    (-1, 1, 144, 16),
+    (1, -1, 160, 16),
+    (1, 1, 176, 16),
 )
 
 
 def face_tables():
-    source = np.full(FACE, -1, np.int64)
-    table = np.zeros((8, FACE), np.int32)
+    pick = np.zeros((2, FACE, ROWS), np.float32)
+    table = np.zeros((8, DATA), np.int32)
     table[1] = DEAD
-    for sx, sy, start, _ in REGIONS:
+    for index, (sx, sy, start, count) in enumerate(REGIONS):
         xs = range(4) if sx == 0 else ((3,) if sx < 0 else (0,))
         ys = range(4) if sy == 0 else ((3,) if sy < 0 else (0,))
         row = start
-        for slot in range(SLOTS):
+        for slot in (0, 2):
             for vx in xs:
                 for vy in ys:
                     for vz in range(4):
-                        source[row] = slot * 64 + vx * 16 + vy * 4 + vz
+                        voxel = vx * 16 + vy * 4 + vz
+                        pick[0, row, slot * 64 + voxel] = 1.0
+                        pick[1, row, (slot or 1) * 64 + voxel] = 1.0
                         table[0, row] = slot
                         table[1, row] = (
                             (8 * sx + vx + 1) * 4096 + (8 * sy + vy + 1) * 64 + vz + 1
                         )
                         row += 1
-        table[2, start : start + (48 if sx * sy == 0 else 16)] = -sx
-        table[3, start : start + (48 if sx * sy == 0 else 16)] = -sy
-    for index, (_, _, start, count) in enumerate(REGIONS):
-        table[4, start : start + count] = index
-    pick = (source[:, None] == np.arange(ROWS)[None, :]).astype(np.float32)
+        region = slice(start, start + count)
+        table[2, region], table[3, region], table[4, region] = -sx, -sy, index
+        table[5, region] = sx != 0
+        table[6, region] = (sx or sy) < 0
     return pick, table
 
 
@@ -154,14 +155,16 @@
 
 
 class Ring:
-    def __init__(self, own, out, inbox, sends, recvs, me, right, left, place):
+    def __init__(self, own, out, inbox, sends, recvs, me, peers, place, direct):
         self.own, self.out, self.inbox = own, out, inbox
         self.sends, self.recvs = sends, recvs
         self.me = place(me)
         self.to_right = place(lax.rem(me + 1, 4))
         self.to_left = place(lax.rem(me + 3, 4))
         across = place(lax.rem(me + 2, 4))
+        right, left, self.far = peers
         self.half = own.shape[1] // 2
+        self.direct = direct
         self.plan = (
             (across, self.half, right),
             (across, 0, left),
@@ -173,6 +176,8 @@
 
     def copy(self, index, piece):
         target, base, peer = self.plan[index]
+        if self.direct(piece) and index < 2:
+            peer = self.far
         return pltpu.make_async_remote_copy(
             src_ref=self.out.at[target, base + piece],
             dst_ref=self.inbox.at[index, piece],
@@ -182,12 +187,14 @@
             device_id_type=MESH,
         )
 
-    def start(self, piece):
-        for index in range(4):
+    def start(self, piece, upper):
+        for index in (0, 3) if upper else (1, 2):
             self.copy(index, piece).start()
+        if self.direct(piece):
+            self.copy(4 if upper else 5, piece).start()
 
     def relay(self, piece):
-        for index in range(2):
+        for index in () if self.direct(piece) else (0, 1):
             target, base, _ = self.plan[4 + index]
             self.copy(index, piece).wait_recv()
             total = self.own[target, base + piece] + self.inbox[index, piece].astype(F32)
@@ -195,13 +202,15 @@
             self.copy(4 + index, piece).start()
 
     def arrive(self, piece):
-        for index in range(2, 6):
+        for index in range(0 if self.direct(piece) else 2, 6):
             self.copy(index, piece).wait_recv()
 
     def total(self, piece, upper):
-        first, second = (3, 4) if upper else (2, 5)
-        mine = self.own[self.me, piece + self.half * upper]
-        return mine + self.inbox[first, piece].astype(F32) + self.inbox[second, piece].astype(F32)
+        total = self.own[self.me, piece + self.half * upper]
+        for index in (3, 4, 0) if upper else (2, 5, 1):
+            if index > 1 or self.direct(piece):
+                total += self.inbox[index, piece].astype(F32)
+        return total
 
     def drain(self):
         for piece in range(self.half):
@@ -257,8 +266,8 @@
     x, y, z, core = chip_place()
     return (
         [device_at(x, y, z, 1 - core)]
-        + [device_at(lax.rem(x + step, 4), y, z, core) for step in (1, 3)]
-        + [device_at(x, lax.rem(y + step, 4), z, core) for step in (1, 3)]
+        + [device_at(lax.rem(x + step, 4), y, z, core) for step in (1, 2, 3)]
+        + [device_at(x, lax.rem(y + step, 4), z, core) for step in (1, 2, 3)]
         + [device_at(x, y, lax.rem(z + step, nz), c) for step in range(1, nz) for c in range(2)]
     )
 
@@ -302,17 +311,22 @@
         x, y, z, core = self.x, self.y, self.z, self.core
         xs, ys, ys2, xs2 = (scratch[5 * i : 5 * i + 5] for i in range(4))
         self.zown, self.zin, self.zout, self.zlate, self.last, self.zsend, self.zrecv = scratch[20:]
-        x_right = device_at(lax.rem(x + 1, 4), y, z, core)
-        x_left = device_at(lax.rem(x + 3, 4), y, z, core)
-        y_right = device_at(x, lax.rem(y + 1, 4), z, core)
-        y_left = device_at(x, lax.rem(y + 3, 4), z, core)
+        along_x = [device_at(lax.rem(x + step, 4), y, z, core) for step in (1, 3, 2)]
+        along_y = [device_at(x, lax.rem(y + step, 4), z, core) for step in (1, 3, 2)]
+
+        def never(piece):
+            return False
+
+        def last(piece):
+            return piece == self.half - 1
+
         self.firsts = [
-            Ring(*xs, x, x_right, x_left, straight),
-            Ring(*ys, y, y_right, y_left, straight),
+            Ring(*xs, x, along_x, straight, never),
+            Ring(*ys, y, along_y, straight, never),
         ]
         self.seconds = [
-            Ring(*ys2, y, y_right, y_left, swapped),
-            Ring(*xs2, x, x_right, x_left, straight),
+            Ring(*ys2, y, along_y, swapped, last),
+            Ring(*xs2, x, along_x, straight, last),
         ]
 
     def advance(self):
@@ -323,37 +337,32 @@
         self.clock += 1
         return self.clock <= self.half + 4
 
-    def begin(self, piece):
-        term = self.term
+    def begin(self, piece, upper):
+        term, z = self.term, piece + upper * self.half
         lane = lax.broadcasted_iota(jnp.int32, (BLOCK, 128), 1)
         even = (lane // 32) % 2 == 0
         below = lane < 64
 
-        def place(ring, target, z, value):
+        def place(ring, target, value):
             ring.own[target, z] = value
             ring.out[target, z] = value.astype(BF16)
 
         ring = self.firsts[0]
-        for z in (piece, piece + self.half):
-            for half in range(2):
-                start = (4 * z + 2 * half) * BLOCK
-                left, right = (
-                    term[start : start + BLOCK, :128],
-                    term[start : start + BLOCK, 128:],
-                )
-                place(ring, 2 * half, z, jnp.where(even, left, pltpu.roll(right, 32, 1)))
-                place(ring, 2 * half + 1, z, jnp.where(even, pltpu.roll(left, 96, 1), right))
-        ring.start(piece)
+        for half in range(2):
+            start = (4 * z + 2 * half) * BLOCK
+            left, right = term[start : start + BLOCK, :128], term[start : start + BLOCK, 128:]
+            place(ring, 2 * half, jnp.where(even, left, pltpu.roll(right, 32, 1)))
+            place(ring, 2 * half + 1, jnp.where(even, pltpu.roll(left, 96, 1), right))
+        ring.start(piece, upper)
         ring = self.firsts[1]
-        for z in (piece, piece + self.half):
-            for pair in range(2):
-                zero, one = (
-                    term[start : start + BLOCK, 128 * pair : 128 * pair + 128]
-                    for start in ((4 * z + 1) * BLOCK, (4 * z + 3) * BLOCK)
-                )
-                place(ring, 2 * pair, z, jnp.where(below, zero, pltpu.roll(one, 64, 1)))
-                place(ring, 2 * pair + 1, z, jnp.where(below, pltpu.roll(zero, 64, 1), one))
-        ring.start(piece)
+        for pair in range(2):
+            zero, one = (
+                term[start : start + BLOCK, 128 * pair : 128 * pair + 128]
+                for start in ((4 * z + 1) * BLOCK, (4 * z + 3) * BLOCK)
+            )
+            place(ring, 2 * pair, jnp.where(below, zero, pltpu.roll(one, 64, 1)))
+            place(ring, 2 * pair + 1, jnp.where(below, pltpu.roll(zero, 64, 1), one))
+        ring.start(piece, upper)
 
     def relay(self, piece):
         for ring in self.firsts:
@@ -369,7 +378,7 @@
                     following.out,
                     piece + upper * self.half,
                 )
-            following.start(piece)
+                following.start(piece, upper)
 
     def turn_relay(self, piece):
         for ring in self.seconds:
@@ -437,14 +446,15 @@
                     self.zcopy(color, to_z, self.core, self.z).wait_send()
 
 
-def gradient_taps(piece, nz):
-    needed = []
-    for index in range(piece + 1):
-        taps = set()
-        for z in (index, index + nz // 2):
-            taps |= set(range(864 * z // C, -(-864 * (z + 1) // C)))
-        needed.append(taps)
-    return sorted(needed[-1].difference(*needed[:-1]))
+def gradient_taps(nz):
+    done, steps = set(), []
+    for piece in range(nz // 2):
+        for upper in range(2):
+            z = piece + upper * (nz // 2)
+            taps = set(range(864 * z // C, -(-864 * (z + 1) // C)))
+            steps.append((piece, upper, sorted(taps - done)))
+            done |= taps
+    return steps
 
 
 def runs(taps):
@@ -479,6 +489,7 @@
     put_sems,
     feat,
     cot,
+    picks,
     pick,
     table,
     w1,
@@ -515,7 +526,7 @@
             (
                 (feat_hbm, feat),
                 (cot_hbm, cot),
-                (pick_hbm, pick),
+                (pick_hbm, picks),
                 (table_hbm, table),
                 (w1_hbm, w1),
                 (w2_hbm, w2),
@@ -530,8 +541,15 @@
     to_x = gx + table[2:3, :]
     to_y = gy + table[3:4, :]
     inside = (to_x >= 0) & (to_x < nx) & (to_y >= 0) & (to_y < ny)
-    sent = table[1:2, :] + by_slot(table[0:1, :], blocks)
-    sent_code[...] = jnp.broadcast_to(jnp.where(inside, sent, DEAD), (8, FACE))
+    corner = coords_ref[0, 0] // 8
+    side = jnp.where(table[5:6, :] == 1, corner // 2, corner % 2)
+    ground = jnp.where(side == table[6:7, :], 0, 1)
+    sent = table[1:2, :] + by_slot(jnp.where(table[0:1, :] == 2, 2, ground), blocks)
+    for sx, sy, start, count in REGIONS:
+        first = (corner // 2 if sx else corner % 2) == (1 if (sx or sy) < 0 else 0)
+        part = slice(start, start + count)
+        pick[part] = jnp.where(first, picks[0, part], picks[1, part])
+    sent_code[...] = jnp.broadcast_to(jnp.where(inside, sent, DEAD), (8, DATA))
     packed[0, 0] = jnp.dot(pick[...], feat[...], preferred_element_type=F32).astype(BF16)
     packed[0, 1] = jnp.dot(pick[...], cot[...], preferred_element_type=F32).astype(BF16)
     faces = [
@@ -548,18 +566,18 @@
     pl.semaphore_wait(barrier, len(peers))
     for copy in code_copies + faces[0] + faces[1]:
         copy.start()
-    lane = lax.broadcasted_iota(jnp.int32, (8, ROWS), 1)
+    lane = lax.broadcasted_iota(jnp.int32, (8, DATA), 1)
     voxel = lane % 64
     own = (voxel // 16 + 1) * 4096 + ((voxel // 4) % 4 + 1) * 64 + voxel % 4 + 1
-    own += by_slot(lane // 64, blocks)
+    own += by_slot(lane // 64 - FACE // 64, blocks)
     live = live_rows(counts_ref)
-    region = jnp.broadcast_to(table[4:5, :], (8, FACE))
+    region = jnp.broadcast_to(table[4:5, :], (8, DATA))
     for copy in code_copies:
         copy.wait_recv()
     got = codes_in[0]
     for index in range(1, 8):
         got = jnp.where(region == index, codes_in[index], got)
-    code = jnp.concatenate([got, own], axis=1)[0:1, :]
+    code = jnp.where(lane < FACE, got, own)[0:1, :]
     build_placing(code, coords_ref, placing)
     for copy in faces[0]:
         copy.wait_recv()
@@ -611,8 +629,8 @@
     both = jnp.concatenate([rows[1 - core], pair_rows[...]], axis=0)
     turned[...] = both.astype(F32).T.astype(BF16)
     reduce = Reduce(nz, scale, term, scratch)
-    for piece in range(nz // 2):
-        for start, stop in runs(gradient_taps(piece, nz)):
+    for piece, upper, taps in gradient_taps(nz):
+        for start, stop in runs(taps):
 
             @pl.when(core == 0)
             def _():
@@ -633,8 +651,9 @@
                         turned[...], window(26 - tap), preferred_element_type=F32
                     )
 
-        reduce.begin(piece)
-        reduce.advance()
+        reduce.begin(piece, upper)
+        if upper:
+            reduce.advance()
     for field in range(2):
         for copy in faces[2 + field]:
             copy.wait_recv()
@@ -729,8 +748,9 @@
             dma((4,)),
             pltpu.VMEM((ROWS, C), BF16),
             pltpu.VMEM((ROWS, C), BF16),
+            pltpu.VMEM((2, FACE, ROWS), BF16),
             pltpu.VMEM((FACE, ROWS), BF16),
-            pltpu.VMEM((8, FACE), jnp.int32),
+            pltpu.VMEM((8, DATA), jnp.int32),
             pltpu.VMEM((27 * C, C), BF16),
             pltpu.VMEM((27 * C, C), BF16),
             dma((6,)),
@@ -738,8 +758,8 @@
             pltpu.VMEM((2, 2, FACE, C), BF16),
             dma((2, 2, 8)),
             dma((2, 2, 8)),
-            pltpu.VMEM((8, FACE), jnp.int32),
-            pltpu.VMEM((8, 8, FACE), jnp.int32),
+            pltpu.VMEM((8, DATA), jnp.int32),
+            pltpu.VMEM((8, 8, DATA), jnp.int32),
             dma((8,)),
             dma((8,)),
             pltpu.VMEM((9, 96 * SLOTS, DATA), BF16),

time: 63.4 us -> 61.8 us (0.975)
  Pallas kernels: 61.9 us -> 60.2 us
    pallas_call x1, Pallas kernels: 60.1 us -> 58.4 us  [per_device(): pl.pallas_call(functools.partial(step_kernel, nz, scale), out_shape=(stru...]
where the time goes in v2:
time: 61.8 us; the launch traced here: 61.6 us
  Pallas kernels  60.2 us (97%)
  between operations  1.45 us (2%)
    pallas_call x1, Pallas kernels, per_device(): pl.pallas_call(functools.partial(step_kernel, nz, scale), out_shape=(stru...  58.4 us
    pallas_call x1, Pallas kernels, per_device(): pl.pallas_call(store_kernel, out_shape=[struct(result.shape, F32) for res...  1.78 us

profile of v2, /device:TPU:97, one launch (start us, length us, event | category | flops | bytes accessed | tf_op | source)
XLA Modules:
  0.0 61.6 jit_solution(8488392635014628350)
XLA Ops:
  1.3 58.4 %step.1 = (f32[192,256]{1,0:T(8,128)}, f32[192,256]{1,0:T(8,128)}, f32[32,216]{1,0:T(8,128)}, f32[32,216]{1,0:T(8,128)}) custom-call(bf16[192,256]{1,0:T(8,128)(2,1)} %bitcast.7, bf16[192,256]{1,0:T(8,128)(2,1)} %bitcast.8, bf16[2,192,192]{2,1,0:T(8,128)(2,1)} %constant.4.clone.pick_hbm, s32[8,384]{1,0:T(8,128)} %constant.5.clone.table_hbm, s32[1,3]{1,0:T(1,128)} %bitcast.9, ...), custom_call_target="tpu_custom_call" | custom-call | tf_op jit(solution)/shard_map/step/pallas_call | solution.py:733
  59.7 1.8 %store.1 = (f32[192,256]{1,0:T(8,128)}, f32[192,256]{1,0:T(8,128)}, f32[32,216]{1,0:T(8,128)}, f32[32,216]{1,0:T(8,128)}) custom-call(f32[192,256]{1,0:T(8,128)} %get-tuple-element.12.refs_0_, f32[192,256]{1,0:T(8,128)} %get-tuple-element.13.refs_1_, f32[32,216]{1,0:T(8,128)} %get-tuple-element.14.refs_2_, f32[32,216]{1,0:T(8,128)} %get-tuple-element.15.refs_3_), custom_call_target="tpu_custom_call" | custom-call | tf_op jit(solution)/shard_map/store/pallas_call | solution.py:781

commit v3 on v2

--- a/solution.py
+++ b/solution.py
@@ -193,8 +193,8 @@
         if self.direct(piece):
             self.copy(4 if upper else 5, piece).start()
 
-    def relay(self, piece):
-        for index in () if self.direct(piece) else (0, 1):
+    def relay(self, piece, indices=(1, 0)):
+        for index in () if self.direct(piece) else indices:
             target, base, _ = self.plan[4 + index]
             self.copy(index, piece).wait_recv()
             total = self.own[target, base + piece] + self.inbox[index, piece].astype(F32)
@@ -364,9 +364,15 @@
             place(ring, 2 * pair + 1, jnp.where(below, pltpu.roll(zero, 64, 1), one))
         ring.start(piece, upper)
 
+    def relay_lower(self, piece):
+        for ring in self.firsts:
+            ring.relay(piece, (1,))
+
     def relay(self, piece):
+        if piece == self.half - 1:
+            self.relay_lower(piece)
         for ring in self.firsts:
-            ring.relay(piece)
+            ring.relay(piece, (0,))
 
     def turn(self, piece):
         for ring, following in zip(self.firsts, self.seconds):
@@ -600,6 +606,11 @@
     gate = jax.nn.sigmoid(pre)
     hidden = jnp.where(live, pre * gate, 0.0).astype(BF16)
     rows[0] = hidden
+
+    @pl.when(core == 0)
+    def _():
+        pair[1].start()
+
     packed[1, 0] = jnp.dot(pick[...], hidden, preferred_element_type=F32).astype(BF16)
     for copy in faces[1]:
         copy.wait_recv()
@@ -609,8 +620,12 @@
     hidden_grad = conv_back(win.at[0, 1], w2)
     pre_grad = jnp.where(live, hidden_grad * gate * (1.0 + pre * (1.0 - gate)), 0.0).astype(BF16)
     rows[1] = pre_grad
+
+    @pl.when(core == 1)
+    def _():
+        pair[1].start()
+
     packed[1, 1] = jnp.dot(pick[...], pre_grad, preferred_element_type=F32).astype(BF16)
-    pair[1].start()
     for copy in faces[2] + faces[3]:
         copy.start()
     for copy in pair:
@@ -654,6 +669,8 @@
         reduce.begin(piece, upper)
         if upper:
             reduce.advance()
+        elif piece:
+            reduce.relay_lower(piece - 1)
     for field in range(2):
         for copy in faces[2 + field]:
             copy.wait_recv()

time: 61.8 us -> 61.6 us (level)
  no operation moved by 1% of the time
where the time goes in v3:
time: 61.6 us; the launch traced here: 61.4 us
  Pallas kernels  60 us (97%)
  between operations  1.45 us (2%)
    pallas_call x1, Pallas kernels, per_device(): pl.pallas_call(functools.partial(step_kernel, nz, scale), out_shape=(stru...  58.2 us
    pallas_call x1, Pallas kernels, per_device(): pl.pallas_call(store_kernel, out_shape=[struct(result.shape, F32) for res...  1.78 us

profile of v3, /device:TPU:97, one launch (start us, length us, event | category | flops | bytes accessed | tf_op | source)
XLA Modules:
  0.0 61.4 jit_solution(11262571908486226622)
XLA Ops:
  1.3 58.2 %step.1 = (f32[192,256]{1,0:T(8,128)}, f32[192,256]{1,0:T(8,128)}, f32[32,216]{1,0:T(8,128)}, f32[32,216]{1,0:T(8,128)}) custom-call(bf16[192,256]{1,0:T(8,128)(2,1)} %bitcast.7, bf16[192,256]{1,0:T(8,128)(2,1)} %bitcast.8, bf16[2,192,192]{2,1,0:T(8,128)(2,1)} %constant.4.clone.pick_hbm, s32[8,384]{1,0:T(8,128)} %constant.5.clone.table_hbm, s32[1,3]{1,0:T(1,128)} %bitcast.9, ...), custom_call_target="tpu_custom_call" | custom-call | tf_op jit(solution)/shard_map/step/pallas_call | solution.py:750
  59.5 1.8 %store.1 = (f32[192,256]{1,0:T(8,128)}, f32[192,256]{1,0:T(8,128)}, f32[32,216]{1,0:T(8,128)}, f32[32,216]{1,0:T(8,128)}) custom-call(f32[192,256]{1,0:T(8,128)} %get-tuple-element.12.refs_0_, f32[192,256]{1,0:T(8,128)} %get-tuple-element.13.refs_1_, f32[32,216]{1,0:T(8,128)} %get-tuple-element.14.refs_2_, f32[32,216]{1,0:T(8,128)} %get-tuple-element.15.refs_3_), custom_call_target="tpu_custom_call" | custom-call | tf_op jit(solution)/shard_map/store/pallas_call | solution.py:798
